TPU v7x, 128 devices: a whole 4x4x4 slice. The times are simulated.
128 devices in a mesh: req: 8 (over y, core), tok: 16 (over x, z).
Axes of the slice: x: 4, y: 4, z: 4, core: 2. Of those that a mesh axis runs over, the one named last changes fastest.
Arguments:
- layer_input: bfloat16 [16384, 2048], P(('req', 'tok')), may hold values from -12 to 12
- q_in: bfloat16 [16384, 2048], P(('req', 'tok')), may hold values from -10 to 10
- k_in: bfloat16 [16384, 2048], P(('req', 'tok')), may hold values from -10 to 10
- v_in: bfloat16 [16384, 2048], P(('req', 'tok')), may hold values from -6 to 6
- segment_ids: int32 [8, 2048], P('req'), may hold values from 0 to 3, never falling along the last dimension, each value on 1 to 1024 neighbouring positions
- lambda_parts: float32 [4, 128], replicated, may hold values from -0.8 to 0.8
- out_weight: bfloat16 [2048, 2048], replicated, may hold values from -0.125 to 0.125
- ffn_gain: float32 [2048], replicated, may hold values from 0.1 to 1.9
- gate_weight: bfloat16 [2048, 5632], P(None, 'req'), may hold values from -0.125 to 0.125
- up_weight: bfloat16 [2048, 5632], P(None, 'req'), may hold values from -0.125 to 0.125
- down_weight: bfloat16 [5632, 2048], P('req'), may hold values from -0.078125 to 0.078125
- next_gain: float32 [2048], replicated, may hold values from 0.1 to 1.9
- qkv_weight: bfloat16 [2048, 6144], P(None, 'req'), may hold values from -0.125 to 0.125
- page_owner: int32 [8, 256], P('req'), may hold values from 0 to 15, as said below
- page_slot: int32 [8, 256], P('req'), may hold values from 0 to 15, as said below
Outputs:
- layer_output: bfloat16 [16384, 2048], P(('req', 'tok'))
- q_next: bfloat16 [16384, 2048], P(('req', 'tok'))
- page_cache: bfloat16 [2048, 8, 4096], P(('req', 'tok'))
Inputs may be any that keep to these rules, and one draw needn't show every extreme that they name: `segment_ids`: segment numbers never fall along a group; each of the 4 prompts of a group has 1 to 1024 tokens, one exactly 1024. `page_owner`: the 16 pages of each device name every device of its request group as owner exactly once. `page_slot`: within a request group every pair of owner and slot is named by exactly one page.
All inputs are finite; a program needn't handle non-finite values.
Results may differ from a plain program's by a relative error of at most 0.017.
Values may be sent and summed in bfloat16 or wider, within the bound.
A program may use at most 192 MiB of HBM per device.

v0:
```python
import math
import jax
import jax.numpy as jnp
from jax import lax
from jax.sharding import PartitionSpec as P

HEADS = 8
PAGE = 8
NEG_FILL = -1e30
LAMBDA_INIT = 0.2
EPSILON = 1e-05
MAX_SEG = 1024


def rms_rows(values):
    return values * lax.rsqrt(jnp.mean(values * values, axis=-1, keepdims=True) + EPSILON)


def lambda_value(lambda_parts):
    first_term = jnp.exp(jnp.sum(lambda_parts[0] * lambda_parts[1]))
    second_term = jnp.exp(jnp.sum(lambda_parts[2] * lambda_parts[3]))
    return first_term - second_term + LAMBDA_INIT


def body(
    layer_input,
    q_in,
    k_in,
    v_in,
    segment_ids,
    lambda_parts,
    out_weight,
    ffn_gain,
    gate_weight,
    up_weight,
    down_weight,
    next_gain,
    qkv_weight,
    page_owner,
    page_slot,
):
    row_count = q_in.shape[0]
    feat_width = q_in.shape[1]
    head_dim = feat_width // (2 * HEADS)
    peer_count = lax.axis_size("tok")
    tok_place = lax.axis_index("tok")
    seg_row = segment_ids[0]
    first_row = tok_place * row_count
    query_places = first_row + jnp.arange(row_count)
    query_segs = lax.dynamic_slice_in_dim(seg_row, first_row, row_count)
    lambda_mix = lambda_value(lambda_parts)
    score_scale = 1.0 / math.sqrt(head_dim)
    query_split = q_in.reshape(row_count, HEADS, 2, head_dim)
    run_max = jnp.full((HEADS, 2, row_count), NEG_FILL, jnp.float32)
    back = -(-(MAX_SEG - 1) // row_count)
    own_kv = jnp.concatenate([k_in, v_in], axis=1)
    pieces = []
    for shift in range(back, 0, -1):
        pairs = [(src_i, src_i + shift) for src_i in range(peer_count - shift)]
        pieces.append(lax.ppermute(own_kv, "tok", perm=pairs))
    pieces.append(own_kv)
    window = jnp.concatenate(pieces, axis=0)
    piece_len = window.shape[0]
    key_rows = window[:, :feat_width]
    value_rows = window[:, feat_width:]
    key_split = key_rows.reshape(piece_len, HEADS, 2, head_dim)
    value_split = value_rows.reshape(piece_len, HEADS, 2 * head_dim)
    key_places = (tok_place - back) * row_count + jnp.arange(piece_len)
    key_segs = jnp.take(seg_row, jnp.clip(key_places, 0, seg_row.shape[0] - 1))
    visible = (
        (key_places[None, :] >= 0)
        & (key_segs[None, :] == query_segs[:, None])
        & (key_places[None, :] <= query_places[:, None])
    )
    scores = (
        jnp.einsum("qhmd,khmd->hmqk", query_split, key_split, preferred_element_type=jnp.float32)
        * score_scale
    )
    scores = jnp.where(visible, scores, NEG_FILL)
    new_max = jnp.maximum(run_max, jnp.max(scores, axis=-1))
    weights = jnp.where(visible, jnp.exp(scores - new_max[..., None]), 0.0)
    totals = jnp.sum(weights, axis=-1)
    weighted = jnp.einsum(
        "hmqk,khe->hmqe",
        weights.astype(jnp.bfloat16),
        value_split,
        preferred_element_type=jnp.float32,
    )
    run_max, totals, weighted = (new_max, totals, weighted)
    map_outputs = weighted / totals[..., None]
    difference = map_outputs[:, 0] - lambda_mix * map_outputs[:, 1]
    head_outputs = rms_rows(difference) * (1.0 - LAMBDA_INIT)
    attention = (
        jnp.transpose(head_outputs, (1, 0, 2)).reshape(row_count, feat_width).astype(jnp.bfloat16)
    )
    residual_mid = (
        layer_input.astype(jnp.float32)
        + jnp.dot(attention, out_weight, preferred_element_type=jnp.float32)
    ).astype(jnp.bfloat16)
    gathered = lax.all_gather(residual_mid, "req", axis=0, tiled=True)
    normed = (rms_rows(gathered.astype(jnp.float32)) * ffn_gain).astype(jnp.bfloat16)
    gate_proj = jnp.dot(normed, gate_weight, preferred_element_type=jnp.float32)
    up_proj = jnp.dot(normed, up_weight, preferred_element_type=jnp.float32)
    hidden = (jax.nn.silu(gate_proj) * up_proj).astype(jnp.bfloat16)
    ffn_own = lax.psum_scatter(
        jnp.dot(hidden, down_weight, preferred_element_type=jnp.float32).astype(jnp.bfloat16),
        "req",
        scatter_dimension=0,
        tiled=True,
    ).astype(jnp.float32)
    layer_output = (residual_mid.astype(jnp.float32) + ffn_own).astype(jnp.bfloat16)
    next_normed = (rms_rows(layer_output.astype(jnp.float32)) * next_gain).astype(jnp.bfloat16)
    projected_cols = jnp.dot(
        lax.all_gather(next_normed, "req", axis=0, tiled=True),
        qkv_weight,
        preferred_element_type=jnp.float32,
    ).astype(jnp.bfloat16)
    projected = lax.all_to_all(projected_cols, "req", split_axis=0, concat_axis=1, tiled=True)
    q_next = projected[:, :feat_width]
    pages_dev = row_count // PAGE
    per_owner = pages_dev // peer_count
    key_values = projected[:, feat_width:].reshape(pages_dev, PAGE, 2 * feat_width)
    owner_all = page_owner[0].reshape(peer_count, pages_dev)
    slot_all = page_slot[0].reshape(peer_count, pages_dev)
    page_numbers = jnp.arange(pages_dev, dtype=jnp.int32)
    my_owners = lax.dynamic_index_in_dim(owner_all, tok_place, 0, keepdims=False)
    send_order = jnp.argsort(my_owners * pages_dev + page_numbers)
    outgoing = key_values[send_order].reshape(peer_count, per_owner, PAGE, 2 * feat_width)
    incoming = lax.all_to_all(outgoing, "tok", split_axis=0, concat_axis=0, tiled=True)
    rank_keys = jnp.where(
        owner_all == tok_place, page_numbers[None, :], pages_dev + page_numbers[None, :]
    )
    chosen_pages = jnp.argsort(rank_keys, axis=1)[:, :per_owner]
    slot_list = jnp.take_along_axis(slot_all, chosen_pages, axis=1).reshape(pages_dev)
    page_cache = (
        jnp.zeros((pages_dev, PAGE, 2 * feat_width), jnp.bfloat16)
        .at[slot_list]
        .set(incoming.reshape(pages_dev, PAGE, 2 * feat_width))
    )
    return (layer_output, q_next, page_cache)


def solution(mesh):
    in_specs = (
        P(("req", "tok"), None),
        P(("req", "tok"), None),
        P(("req", "tok"), None),
        P(("req", "tok"), None),
        P("req", None),
        P(),
        P(),
        P(),
        P(None, "req"),
        P(None, "req"),
        P("req", None),
        P(),
        P(None, "req"),
        P("req", None),
        P("req", None),
    )
    out_specs = (P(("req", "tok"), None), P(("req", "tok"), None), P(("req", "tok"), None, None))
    return jax.shard_map(body, mesh=mesh, in_specs=in_specs, out_specs=out_specs, check_vma=False)
```

profile of v0, /device:TPU:0, one launch (start us, length us, event | category | flops | bytes accessed | tf_op | source)
XLA Modules:
  0.0 437.3 jit_solution(304008285303600586)
XLA Ops:
  13.7 6.0 %collective-permute-start = (bf16[128,4096]{0,1:T(8,128)(2,1)}, bf16[128,4096]{0,1:T(8,128)(2,1)}, u32[]{:S(2)}, u32[]{:S(2)}) collective-permute-start(bf16[128,4096]{0,1:T(8,128)(2,1)} %pad_maximum_fusion), channel_id=1, source_target_pairs={{0,8},{1,9},{2,10},{3,11},{4,12},{5,13},{6,14},{7,15},{16,24},{17,... | collective-permute-start | bytes 3145736 | tf_op jit(solution)/shard_map/ppermute | solution.py:60
  19.7 7.0 %collective-permute-start.1 = (bf16[128,4096]{0,1:T(8,128)(2,1)}, bf16[128,4096]{0,1:T(8,128)(2,1)}, u32[]{:S(2)}, u32[]{:S(2)}) collective-permute-start(bf16[128,4096]{0,1:T(8,128)(2,1)} %pad_maximum_fusion), channel_id=1, source_target_pairs={{0,7},{1,8},{2,9},{3,10},{4,11},{5,12},{6,13},{7,14},{8,15},{16,23... | collective-permute-start | bytes 3145736 | tf_op jit(solution)/shard_map/ppermute | solution.py:60
  33.6 6.5 %gather_fusion = s32[1152]{0:T(1024)S(1)} fusion(s32[2048]{0:T(1024)S(1)} %bitcast.62, s32[2048]{0:T(1024)S(1)} %pad_clamp_fusion), kind=kCustom, calls=%fused_computation | custom fusion | bytes 13824 | tf_op jit(solution)/shard_map/jit(_take)/gather | solution.py:69
  45.4 3.2 collective-permute-start.5
  48.6 2.4 constant_dynamic-update-slice_fusion.8
  51.0 14.2 %collective-permute-done.1 = bf16[128,4096]{0,1:T(8,128)(2,1)} collective-permute-done((bf16[128,4096]{0,1:T(8,128)(2,1)}, bf16[128,4096]{0,1:T(8,128)(2,1)}, u32[]{:S(2)}, u32[]{:S(2)}) %collective-permute-start.1) | collective-permute-done | bytes 1048608 | tf_op jit(solution)/shard_map/ppermute | solution.py:60
  65.1 5.8 %collective-permute-start.6 = (bf16[128,4096]{0,1:T(8,128)(2,1)}, bf16[128,4096]{0,1:T(8,128)(2,1)S(1)}, u32[]{:S(2)}, u32[]{:S(2)}) collective-permute-start(bf16[128,4096]{0,1:T(8,128)(2,1)} %pad_maximum_fusion), channel_id=1, source_target_pairs={{0,2},{1,3},{2,4},{3,5},{4,6},{5,7},{6,8},{7,9},{8,10},{9,11},{10,... | collective-permute-start | bytes 3145736 | tf_op jit(solution)/shard_map/ppermute | solution.py:60
  70.9 2.3 constant_dynamic-update-slice_fusion.7
  73.3 14.4 %collective-permute-done.2 = bf16[128,4096]{0,1:T(8,128)(2,1)} collective-permute-done((bf16[128,4096]{0,1:T(8,128)(2,1)}, bf16[128,4096]{0,1:T(8,128)(2,1)}, u32[]{:S(2)}, u32[]{:S(2)}) %collective-permute-start.2) | collective-permute-done | bytes 1048608 | tf_op jit(solution)/shard_map/ppermute | solution.py:60
  87.6 4.0 collective-permute-start.7
  91.7 2.4 constant_dynamic-update-slice_fusion.6
  94.0 16.1 %collective-permute-done.3 = bf16[128,4096]{0,1:T(8,128)(2,1)} collective-permute-done((bf16[128,4096]{0,1:T(8,128)(2,1)}, bf16[128,4096]{0,1:T(8,128)(2,1)}, u32[]{:S(2)}, u32[]{:S(2)}) %collective-permute-start.3) | collective-permute-done | bytes 1048608 | tf_op jit(solution)/shard_map/ppermute | solution.py:60
  110.1 2.4 constant_dynamic-update-slice_fusion.5
  112.5 19.0 %collective-permute-done.4 = bf16[128,4096]{0,1:T(8,128)(2,1)} collective-permute-done((bf16[128,4096]{0,1:T(8,128)(2,1)}, bf16[128,4096]{0,1:T(8,128)(2,1)}, u32[]{:S(2)}, u32[]{:S(2)}) %collective-permute-start.4) | collective-permute-done | bytes 1048608 | tf_op jit(solution)/shard_map/ppermute | solution.py:60
  131.4 2.4 constant_dynamic-update-slice_fusion.4
  138.3 6.8 %fusion.37 = (bf16[1152,2048]{0,1:T(8,128)(2,1)}, bf16[1152,2048]{0,1:T(8,128)(2,1)S(1)}) fusion(bf16[1152,4096]{0,1:T(8,128)(2,1)} %constant_dynamic-update-slice_fusion), kind=kLoop, calls=%fused_computation.84 | loop fusion | bytes 18874368 | tf_op jit(solution)/shard_map/slice | solution.py:65
  145.1 2.5 fusion.3
  151.2 8.3 %broadcast_divide_fusion = f32[8,2,128,256]{3,2,1,0:T(8,128)S(1)} fusion(f32[8,2,128]{2,1,0:T(2,128)S(1)} %fusion.4, bf16[1152,8,256,1]{0,2,3,1:T(8,128)(2,1)} %bitcast.66, f32[8,2,1152,128]{3,2,1,0:T(8,128)} %copy-done.2, f32[8,2,128]{2,1,0:T(2,128)S(1)} %broadcast_maximum_fusion, pred[128,1152]{0,1:T(8,128)(4,1)S(1)} %compare_and_fusion), kind=kOutput, calls=%fused_computation.39 | convolution fusion | flops 1220280320 | bytes 16416768 | tf_op jit(solution)/shard_map/hmqk,khe->hmqe/dot_general | solution.py:83
  162.9 5.7 %fusion.13 = bf16[128,2048]{1,0:T(8,128)(2,1)} fusion(bf16[128,2048]{0,1:T(8,128)(2,1)} %bitcast.68, bf16[2048,2048]{1,0:T(8,128)(2,1)} %param.21, bf16[128,2048]{1,0:T(8,128)(2,1)} %param.15), kind=kOutput, calls=%fused_computation.23 | convolution fusion | flops 1074528256 | bytes 9961472 | tf_op jit(solution)/shard_map/dot_general | solution.py:98
  168.8 97.9 %all-gather.3.cloned.1.call-done = bf16[1024,2048]{1,0:T(8,128)(2,1)} async-done(((bf16[128,2048]{1,0:T(8,128)(2,1)}), bf16[1024,2048]{1,0:T(8,128)(2,1)}) %all-gather.3.cloned.1.call-update) | async-done | bytes 4194320 | tf_op jit(solution)/shard_map/all_gather | solution.py:100
  266.7 3.1 fusion
  269.8 8.0 %fusion.15 = f32[1024,704]{0,1:T(8,128)} fusion(bf16[2048,704]{0,1:T(8,128)(2,1)} %param.23, bf16[1024,2048]{1,0:T(8,128)(2,1)} %all-gather.3.cloned.1.call-done, f32[2048]{0:T(1024)S(1)} %copy-done.12, f32[1024]{0:T(1024)S(1)} %add_rsqrt_fusion), kind=kOutput, calls=%fused_computation.27 | convolution fusion | flops 2961178624 | bytes 9973760 | tf_op jit(solution)/shard_map/dot_general | solution.py:102
  277.8 12.4 %convolution_convert_fusion = bf16[1024,2048]{1,0:T(8,128)(2,1)} fusion(bf16[704,2048]{1,0:T(8,128)(2,1)} %param.25, f32[1024,704]{0,1:T(8,128)} %fusion.15, bf16[2048,704]{0,1:T(8,128)(2,1)} %param.24, bf16[1024,2048]{1,0:T(8,128)(2,1)} %all-gather.3.cloned.1.call-done, f32[2048]{0:T(1024)S(1)} %copy-done.12, f32[1024]{0:T(1024)S(1)} %add_rsqrt_fusion), kind=kOutput, calls=%fused_computation.20 | convolution fusion | flops 5920391168 | bytes 17051648 | tf_op jit(solution)/shard_map/dot_general | solution.py:106
  290.3 37.9 %reduce-scatter.2.cloned.1.call-done = bf16[128,2048]{1,0:T(8,128)(2,1)} async-done(((bf16[1024,2048]{1,0:T(8,128)(2,1)}), bf16[128,2048]{1,0:T(8,128)(2,1)}) %reduce-scatter.2.cloned.1.call-update) | async-done | bytes 524304 | tf_op jit(solution)/shard_map/reduce_scatter | solution.py:105
  331.4 31.2 %all-gather.5.cloned.1.call-done = bf16[1024,2048]{1,0:T(8,128)(2,1)} async-done(((bf16[128,2048]{1,0:T(8,128)(2,1)}), bf16[1024,2048]{1,0:T(8,128)(2,1)}) %all-gather.5.cloned.1.call-update) | async-done | bytes 4194320 | tf_op jit(solution)/shard_map/all_gather | solution.py:114
  362.6 6.8 %convolution_convert_fusion.1 = bf16[1024,768]{1,0:T(8,128)(2,1)} fusion(bf16[1024,2048]{1,0:T(8,128)(2,1)} %all-gather.5.cloned.1.call-done, bf16[2048,768]{1,0:T(8,128)(2,1)S(1)} %copy-done), kind=kOutput, calls=%fused_computation.24 | convolution fusion | flops 3222011904 | bytes 8912896 | tf_op jit(solution)/shard_map/dot_general | solution.py:113
  369.4 4.3 all-to-all-start
  377.0 18.2 %all-to-all-done = bf16[8,128,768]{2,1,0:T(8,128)(2,1)} async-done(((bf16[8,128,768]{2,1,0:T(8,128)(2,1)}), bf16[8,128,768]{2,1,0:T(8,128)(2,1)}, u32[]{:S(2)}, u32[]{:S(2)}) %all-to-all-start) | async-done | bytes 1572896 | tf_op jit(solution)/shard_map/all_to_all | solution.py:118
  399.0 2.8 gather_fusion.1
  401.8 7.0 %all-to-all-start.1 = ((bf16[16,1,8,4096]{3,2,1,0:T(8,128)(2,1)}), bf16[16,1,8,4096]{3,2,1,0:T(8,128)(2,1)}, u32[]{:S(2)}, u32[]{:S(2)}) async-start(bf16[16,1,8,4096]{3,2,1,0:T(8,128)(2,1)} %bitcast.67), calls=%async_computation.2 | async-start | bytes 2097152 | tf_op jit(solution)/shard_map/all_to_all | solution.py:129
  412.2 14.1 %all-to-all-done.1 = bf16[16,1,8,4096]{3,2,1,0:T(8,128)(2,1)} async-done(((bf16[16,1,8,4096]{3,2,1,0:T(8,128)(2,1)}), bf16[16,1,8,4096]{3,2,1,0:T(8,128)(2,1)}, u32[]{:S(2)}, u32[]{:S(2)}) %all-to-all-start.1) | async-done | bytes 1048608 | tf_op jit(solution)/shard_map/all_to_all | solution.py:129
  427.4 3.4 scatter_fusion
  (90 shorter events, 43.9 us)
Async XLA Ops:
  7.2 355.4 %copy-start = (bf16[2048,768]{1,0:T(8,128)(2,1)S(1)}, bf16[2048,768]{1,0:T(8,128)(2,1)}, u32[]{:S(2)}) copy-start(bf16[2048,768]{1,0:T(8,128)(2,1)} %param.27) | copy-start | bytes 9437188
  7.2 26.4 %copy-start.1 = (s32[1,2048]{1,0:T(1,128)S(1)}, s32[1,2048]{1,0:T(1,128)}, u32[]{:S(2)}) copy-start(s32[1,2048]{1,0:T(1,128)} %param.19) | copy-start | bytes 24580
  7.2 259.5 %all-gather.3.cloned.1.call-start = ((), (), s32[]{:S(2)}) async-start(), calls=%async_computation.3 | async-start | bytes 4718592 | tf_op jit(solution)/shard_map/all_gather | solution.py:100
  13.7 31.7 %collective-permute-start = (bf16[128,4096]{0,1:T(8,128)(2,1)}, bf16[128,4096]{0,1:T(8,128)(2,1)}, u32[]{:S(2)}, u32[]{:S(2)}) collective-permute-start(bf16[128,4096]{0,1:T(8,128)(2,1)} %pad_maximum_fusion), channel_id=1, source_target_pairs={{0,8},{1,9},{2,10},{3,11},{4,12},{5,13},{6,14},{7,15},{16,24},{17,... | collective-permute-start | bytes 3145736 | tf_op jit(solution)/shard_map/ppermute | solution.py:60
  19.7 45.4 %collective-permute-start.1 = (bf16[128,4096]{0,1:T(8,128)(2,1)}, bf16[128,4096]{0,1:T(8,128)(2,1)}, u32[]{:S(2)}, u32[]{:S(2)}) collective-permute-start(bf16[128,4096]{0,1:T(8,128)(2,1)} %pad_maximum_fusion), channel_id=1, source_target_pairs={{0,7},{1,8},{2,9},{3,10},{4,11},{5,12},{6,13},{7,14},{8,15},{16,23... | collective-permute-start | bytes 3145736 | tf_op jit(solution)/shard_map/ppermute | solution.py:60
  26.7 60.9 %collective-permute-start.2 = (bf16[128,4096]{0,1:T(8,128)(2,1)}, bf16[128,4096]{0,1:T(8,128)(2,1)}, u32[]{:S(2)}, u32[]{:S(2)}) collective-permute-start(bf16[128,4096]{0,1:T(8,128)(2,1)} %pad_maximum_fusion), channel_id=1, source_target_pairs={{0,6},{1,7},{2,8},{3,9},{4,10},{5,11},{6,12},{7,13},{8,14},{9,15},... | collective-permute-start | bytes 3145736 | tf_op jit(solution)/shard_map/ppermute | solution.py:60
  29.0 81.2 %collective-permute-start.3 = (bf16[128,4096]{0,1:T(8,128)(2,1)}, bf16[128,4096]{0,1:T(8,128)(2,1)}, u32[]{:S(2)}, u32[]{:S(2)}) collective-permute-start(bf16[128,4096]{0,1:T(8,128)(2,1)} %pad_maximum_fusion), channel_id=1, source_target_pairs={{0,5},{1,6},{2,7},{3,8},{4,9},{5,10},{6,11},{7,12},{8,13},{9,14},{... | collective-permute-start | bytes 3145736 | tf_op jit(solution)/shard_map/ppermute | solution.py:60
  31.2 100.2 %collective-permute-start.4 = (bf16[128,4096]{0,1:T(8,128)(2,1)}, bf16[128,4096]{0,1:T(8,128)(2,1)}, u32[]{:S(2)}, u32[]{:S(2)}) collective-permute-start(bf16[128,4096]{0,1:T(8,128)(2,1)} %pad_maximum_fusion), channel_id=1, source_target_pairs={{0,4},{1,5},{2,6},{3,7},{4,8},{5,9},{6,10},{7,11},{8,12},{9,13},{1... | collective-permute-start | bytes 3145736 | tf_op jit(solution)/shard_map/ppermute | solution.py:60
  33.6 9.8 %copy-start.9 = (f32[4,128]{1,0:T(4,128)S(1)}, f32[4,128]{1,0:T(4,128)}, u32[]{:S(2)}) copy-start(f32[4,128]{1,0:T(4,128)} %param.20) | copy-start | bytes 6148
  45.4 88.4 %collective-permute-start.5 = (bf16[128,4096]{0,1:T(8,128)(2,1)}, bf16[128,4096]{0,1:T(8,128)(2,1)S(1)}, u32[]{:S(2)}, u32[]{:S(2)}) collective-permute-start(bf16[128,4096]{0,1:T(8,128)(2,1)} %pad_maximum_fusion), channel_id=1, source_target_pairs={{0,3},{1,4},{2,5},{3,6},{4,7},{5,8},{6,9},{7,10},{8,11},{9,12},{10... | collective-permute-start | bytes 3145736 | tf_op jit(solution)/shard_map/ppermute | solution.py:60
  65.1 69.8 %collective-permute-start.6 = (bf16[128,4096]{0,1:T(8,128)(2,1)}, bf16[128,4096]{0,1:T(8,128)(2,1)S(1)}, u32[]{:S(2)}, u32[]{:S(2)}) collective-permute-start(bf16[128,4096]{0,1:T(8,128)(2,1)} %pad_maximum_fusion), channel_id=1, source_target_pairs={{0,2},{1,3},{2,4},{3,5},{4,6},{5,7},{6,8},{7,9},{8,10},{9,11},{10,... | collective-permute-start | bytes 3145736 | tf_op jit(solution)/shard_map/ppermute | solution.py:60
  87.6 48.4 %collective-permute-start.7 = (bf16[128,4096]{0,1:T(8,128)(2,1)}, bf16[128,4096]{0,1:T(8,128)(2,1)S(1)}, u32[]{:S(2)}, u32[]{:S(2)}) collective-permute-start(bf16[128,4096]{0,1:T(8,128)(2,1)} %pad_maximum_fusion), channel_id=1, source_target_pairs={{0,1},{1,2},{2,3},{3,4},{4,5},{5,6},{6,7},{7,8},{8,9},{9,10},{10,1... | collective-permute-start | bytes 3145736 | tf_op jit(solution)/shard_map/ppermute | solution.py:60
  112.5 24.7 %copy-start.4 = (bf16[128,2048]{0,1:T(8,128)(2,1)S(1)}, bf16[128,2048]{0,1:T(8,128)(2,1)}, u32[]{:S(2)}) copy-start(bf16[128,2048]{0,1:T(8,128)(2,1)} %copy.38) | copy-start | bytes 1572868
  112.5 24.7 %copy-start.5 = (bf16[128,2048]{0,1:T(8,128)(2,1)S(1)}, bf16[128,2048]{0,1:T(8,128)(2,1)}, u32[]{:S(2)}) copy-start(bf16[128,2048]{0,1:T(8,128)(2,1)} %copy.39) | copy-start | bytes 1572868
  138.3 6.8 %copy-start.6 = (bf16[128,8,2,128]{3,2,1,0:T(2,128)(2,1)S(1)}, bf16[128,8,2,128]{3,2,1,0:T(2,128)(2,1)}, u32[]{:S(2)}) copy-start(bf16[128,8,2,128]{3,2,1,0:T(2,128)(2,1)} %reshape.141) | copy-start | bytes 1572868
  147.6 3.6 copy-start.2
  168.5 101.3 %copy-start.12 = (f32[2048]{0:T(1024)S(1)}, f32[2048]{0:T(1024)}, u32[]{:S(2)}) copy-start(f32[2048]{0:T(1024)} %param.22) | copy-start | bytes 24580
  168.5 159.6 %reduce-scatter.2.cloned.1.call-start = ((), (), s32[]{:S(2)}) async-start(), calls=%async_computation.4 | async-start | bytes 4718592 | tf_op jit(solution)/shard_map/reduce_scatter | solution.py:105
  290.2 40.2 %copy-start.8 = (f32[2048]{0:T(1024)S(1)}, f32[2048]{0:T(1024)}, u32[]{:S(2)}) copy-start(f32[2048]{0:T(1024)} %param.26) | copy-start | bytes 24580
  290.2 72.4 %all-gather.5.cloned.1.call-start = ((), (), s32[]{:S(2)}) async-start(), calls=%async_computation.5 | async-start | bytes 4718592 | tf_op jit(solution)/shard_map/all_gather | solution.py:114
  329.6 0.8 copy-start.7
  331.4 42.8 %copy-start.10 = (s32[1,256]{1,0:T(1,128)S(1)}, s32[1,256]{1,0:T(1,128)}, u32[]{:S(2)}) copy-start(s32[1,256]{1,0:T(1,128)} %param.28) | copy-start | bytes 3076
  331.4 43.6 %copy-start.11 = (s32[1,256]{1,0:T(1,128)S(1)}, s32[1,256]{1,0:T(1,128)}, u32[]{:S(2)}) copy-start(s32[1,256]{1,0:T(1,128)} %param.29) | copy-start | bytes 3076
  369.4 25.9 %all-to-all-start = ((bf16[8,128,768]{2,1,0:T(8,128)(2,1)}), bf16[8,128,768]{2,1,0:T(8,128)(2,1)}, u32[]{:S(2)}, u32[]{:S(2)}) async-start(bf16[8,128,768]{2,1,0:T(8,128)(2,1)} %bitcast.69), calls=%async_computation.1 | async-start | bytes 3145728 | tf_op jit(solution)/shard_map/all_to_all | solution.py:118
  396.8 1.2 copy-start.3
  401.8 24.4 %all-to-all-start.1 = ((bf16[16,1,8,4096]{3,2,1,0:T(8,128)(2,1)}), bf16[16,1,8,4096]{3,2,1,0:T(8,128)(2,1)}, u32[]{:S(2)}, u32[]{:S(2)}) async-start(bf16[16,1,8,4096]{3,2,1,0:T(8,128)(2,1)} %bitcast.67), calls=%async_computation.2 | async-start | bytes 2097152 | tf_op jit(solution)/shard_map/all_to_all | solution.py:129
Sparse Core Ops, SparseCore 0:
  168.7 98.0 all-gather.2
  290.4 37.7 reduce-scatter.1
  331.5 31.0 all-gather.4
where the time goes:
time: 438 us; the launch traced here: 437 us
  waiting for transfers between devices  263 us (60%)
  local copies, waits for them, and re-layouts  53.4 us (12%)
  starting transfers between devices  44.4 us (10%)
  matrix products  43.6 us (10%)
  other arithmetic  17.7 us (4%)
  between operations  15.4 us (4%)
    all_gather x1, waiting for transfers between devices, body(): gathered = lax.all_gather(residual_mid, 'req', axis=0, tiled=True)  97.9 us
    ppermute x8, waiting for transfers between devices, body(): pieces.append(lax.ppermute(own_kv, 'tok', perm=pairs))  63.6 us
    reduce_scatter x1, waiting for transfers between devices, body(): lax.psum_scatter(jnp.dot(hidden, down_weight, preferred_element_type=jnp....  37.9 us
    ppermute x8, starting transfers between devices, body(): pieces.append(lax.ppermute(own_kv, 'tok', perm=pairs))  32.8 us
    all_gather x1, waiting for transfers between devices, body(): lax.all_gather(next_normed, 'req', axis=0, tiled=True)  31.2 us
    unnamed x38, local copies, waits for them, and re-layouts  23.2 us
    all_to_all x1, waiting for transfers between devices, body(): lax.all_to_all(projected_cols, 'req', split_axis=0, concat_axis=1, tiled=...  18.2 us
    all_to_all x1, waiting for transfers between devices, body(): lax.all_to_all(outgoing, 'tok', split_axis=0, concat_axis=0, tiled=True)  14.1 us
  transfers between devices with their start and end apart: 13, of which 9 were waited for; matrix products, arithmetic and copies ran while one was open for 7% of the time, Pallas kernels for 0%

commit v1 on v0

--- a/solution.py
+++ b/solution.py
@@ -111,7 +111,9 @@
     layer_output = (residual_mid.astype(jnp.float32) + ffn_own).astype(jnp.bfloat16)
     next_normed = (rms_rows(layer_output.astype(jnp.float32)) * next_gain).astype(jnp.bfloat16)
     projected_cols = jnp.dot(
-        lax.all_gather(next_normed, "req", axis=0, tiled=True),
+        jnp.concatenate(
+            lax.all_to_all(jnp.stack([next_normed] * lax.axis_size("req")), "req", 0, 0), axis=0
+        ),
         qkv_weight,
         preferred_element_type=jnp.float32,
     ).astype(jnp.bfloat16)

time: 438 us -> 458 us (1.046)
  blocking collectives: 0 us -> 52.8 us
  waiting for transfers between devices: 263 us -> 232 us
    all_to_all x0 -> x1, blocking collectives: none -> 52.8 us  [body(): lax.all_to_all(jnp.stack([next_normed] * lax.axis_size('req')), 'req', 0, 0)]
    all_gather x1 -> x0, waiting for transfers between devices: 31.2 us -> none  [body(): lax.all_gather(next_normed, 'req', axis=0, tiled=True)]
  transfers between devices with their start and end apart: 13 -> 12, of which waited for: 9 -> 8; matrix products, arithmetic and copies ran while one was open for 7% -> 7% of each run, Pallas kernels for 0% -> 0%
where the time goes in v1:
time: 458 us; the launch traced here: 457 us
  waiting for transfers between devices  232 us (51%)
  local copies, waits for them, and re-layouts  53.9 us (12%)
  blocking collectives  52.8 us (12%)
  starting transfers between devices  44.4 us (10%)
  matrix products  41.3 us (9%)
  other arithmetic  16.9 us (4%)
  between operations  15.7 us (3%)
    all_gather x1, waiting for transfers between devices, body(): gathered = lax.all_gather(residual_mid, 'req', axis=0, tiled=True)  97.9 us
    ppermute x8, waiting for transfers between devices, body(): pieces.append(lax.ppermute(own_kv, 'tok', perm=pairs))  63.6 us
    all_to_all x1, blocking collectives, body(): lax.all_to_all(jnp.stack([next_normed] * lax.axis_size('req')), 'req', 0, 0)  52.8 us
    reduce_scatter x1, waiting for transfers between devices, body(): lax.psum_scatter(jnp.dot(hidden, down_weight, preferred_element_type=jnp....  37.9 us
    ppermute x8, starting transfers between devices, body(): pieces.append(lax.ppermute(own_kv, 'tok', perm=pairs))  32.8 us
    unnamed x38, local copies, waits for them, and re-layouts  23.2 us
    all_to_all x1, waiting for transfers between devices, body(): lax.all_to_all(projected_cols, 'req', split_axis=0, concat_axis=1, tiled=...  18.2 us
    all_to_all x1, waiting for transfers between devices, body(): lax.all_to_all(outgoing, 'tok', split_axis=0, concat_axis=0, tiled=True)  14.1 us
  transfers between devices with their start and end apart: 12, of which 8 were waited for; matrix products, arithmetic and copies ran while one was open for 7% of the time, Pallas kernels for 0%

profile of v1, /device:TPU:0, one launch (start us, length us, event | category | flops | bytes accessed | tf_op | source)
XLA Modules:
  0.0 456.7 jit_solution(14254652004962880247)
XLA Ops:
  13.7 6.0 %collective-permute-start = (bf16[128,4096]{0,1:T(8,128)(2,1)}, bf16[128,4096]{0,1:T(8,128)(2,1)}, u32[]{:S(2)}, u32[]{:S(2)}) collective-permute-start(bf16[128,4096]{0,1:T(8,128)(2,1)} %pad_maximum_fusion), channel_id=1, source_target_pairs={{0,8},{1,9},{2,10},{3,11},{4,12},{5,13},{6,14},{7,15},{16,24},{17,... | collective-permute-start | bytes 3145736 | tf_op jit(solution)/shard_map/ppermute | solution.py:60
  19.7 7.0 %collective-permute-start.1 = (bf16[128,4096]{0,1:T(8,128)(2,1)}, bf16[128,4096]{0,1:T(8,128)(2,1)}, u32[]{:S(2)}, u32[]{:S(2)}) collective-permute-start(bf16[128,4096]{0,1:T(8,128)(2,1)} %pad_maximum_fusion), channel_id=1, source_target_pairs={{0,7},{1,8},{2,9},{3,10},{4,11},{5,12},{6,13},{7,14},{8,15},{16,23... | collective-permute-start | bytes 3145736 | tf_op jit(solution)/shard_map/ppermute | solution.py:60
  33.6 6.5 %gather_fusion = s32[1152]{0:T(1024)S(1)} fusion(s32[2048]{0:T(1024)S(1)} %bitcast.63, s32[2048]{0:T(1024)S(1)} %pad_clamp_fusion), kind=kCustom, calls=%fused_computation | custom fusion | bytes 13824 | tf_op jit(solution)/shard_map/jit(_take)/gather | solution.py:69
  45.4 3.2 collective-permute-start.5
  48.6 2.4 constant_dynamic-update-slice_fusion.8
  51.0 14.2 %collective-permute-done.1 = bf16[128,4096]{0,1:T(8,128)(2,1)} collective-permute-done((bf16[128,4096]{0,1:T(8,128)(2,1)}, bf16[128,4096]{0,1:T(8,128)(2,1)}, u32[]{:S(2)}, u32[]{:S(2)}) %collective-permute-start.1) | collective-permute-done | bytes 1048608 | tf_op jit(solution)/shard_map/ppermute | solution.py:60
  65.1 5.8 %collective-permute-start.6 = (bf16[128,4096]{0,1:T(8,128)(2,1)}, bf16[128,4096]{0,1:T(8,128)(2,1)S(1)}, u32[]{:S(2)}, u32[]{:S(2)}) collective-permute-start(bf16[128,4096]{0,1:T(8,128)(2,1)} %pad_maximum_fusion), channel_id=1, source_target_pairs={{0,2},{1,3},{2,4},{3,5},{4,6},{5,7},{6,8},{7,9},{8,10},{9,11},{10,... | collective-permute-start | bytes 3145736 | tf_op jit(solution)/shard_map/ppermute | solution.py:60
  70.9 2.3 constant_dynamic-update-slice_fusion.7
  73.3 14.4 %collective-permute-done.2 = bf16[128,4096]{0,1:T(8,128)(2,1)} collective-permute-done((bf16[128,4096]{0,1:T(8,128)(2,1)}, bf16[128,4096]{0,1:T(8,128)(2,1)}, u32[]{:S(2)}, u32[]{:S(2)}) %collective-permute-start.2) | collective-permute-done | bytes 1048608 | tf_op jit(solution)/shard_map/ppermute | solution.py:60
  87.6 4.0 collective-permute-start.7
  91.7 2.4 constant_dynamic-update-slice_fusion.6
  94.0 16.1 %collective-permute-done.3 = bf16[128,4096]{0,1:T(8,128)(2,1)} collective-permute-done((bf16[128,4096]{0,1:T(8,128)(2,1)}, bf16[128,4096]{0,1:T(8,128)(2,1)}, u32[]{:S(2)}, u32[]{:S(2)}) %collective-permute-start.3) | collective-permute-done | bytes 1048608 | tf_op jit(solution)/shard_map/ppermute | solution.py:60
  110.1 2.4 constant_dynamic-update-slice_fusion.5
  112.5 19.0 %collective-permute-done.4 = bf16[128,4096]{0,1:T(8,128)(2,1)} collective-permute-done((bf16[128,4096]{0,1:T(8,128)(2,1)}, bf16[128,4096]{0,1:T(8,128)(2,1)}, u32[]{:S(2)}, u32[]{:S(2)}) %collective-permute-start.4) | collective-permute-done | bytes 1048608 | tf_op jit(solution)/shard_map/ppermute | solution.py:60
  131.4 2.4 constant_dynamic-update-slice_fusion.4
  138.3 6.8 %fusion.37 = (bf16[1152,2048]{0,1:T(8,128)(2,1)}, bf16[1152,2048]{0,1:T(8,128)(2,1)S(1)}) fusion(bf16[1152,4096]{0,1:T(8,128)(2,1)} %constant_dynamic-update-slice_fusion), kind=kLoop, calls=%fused_computation.84 | loop fusion | bytes 18874368 | tf_op jit(solution)/shard_map/slice | solution.py:65
  145.1 2.5 fusion.3
  151.2 8.3 %broadcast_divide_fusion = f32[8,2,128,256]{3,2,1,0:T(8,128)S(1)} fusion(f32[8,2,128]{2,1,0:T(2,128)S(1)} %fusion.4, bf16[1152,8,256,1]{0,2,3,1:T(8,128)(2,1)} %bitcast.67, f32[8,2,1152,128]{3,2,1,0:T(8,128)} %copy-done.2, f32[8,2,128]{2,1,0:T(2,128)S(1)} %broadcast_maximum_fusion, pred[128,1152]{0,1:T(8,128)(4,1)S(1)} %compare_and_fusion), kind=kOutput, calls=%fused_computation.39 | convolution fusion | flops 1220280320 | bytes 16416768 | tf_op jit(solution)/shard_map/hmqk,khe->hmqe/dot_general | solution.py:83
  162.9 5.7 %fusion.13 = bf16[128,2048]{1,0:T(8,128)(2,1)} fusion(bf16[128,2048]{0,1:T(8,128)(2,1)} %bitcast.70, bf16[2048,2048]{1,0:T(8,128)(2,1)} %param.21, bf16[128,2048]{1,0:T(8,128)(2,1)} %param.15), kind=kOutput, calls=%fused_computation.23 | convolution fusion | flops 1074528256 | bytes 9961472 | tf_op jit(solution)/shard_map/dot_general | solution.py:98
  168.8 97.9 %all-gather.2.cloned.1.call-done = bf16[1024,2048]{1,0:T(8,128)(2,1)} async-done(((bf16[128,2048]{1,0:T(8,128)(2,1)}), bf16[1024,2048]{1,0:T(8,128)(2,1)}) %all-gather.2.cloned.1.call-update) | async-done | bytes 4194320 | tf_op jit(solution)/shard_map/all_gather | solution.py:100
  266.7 3.1 fusion
  269.8 8.0 %fusion.15 = f32[1024,704]{0,1:T(8,128)} fusion(bf16[2048,704]{0,1:T(8,128)(2,1)} %param.23, bf16[1024,2048]{1,0:T(8,128)(2,1)} %all-gather.2.cloned.1.call-done, f32[2048]{0:T(1024)S(1)} %copy-done.12, f32[1024]{0:T(1024)S(1)} %add_rsqrt_fusion), kind=kOutput, calls=%fused_computation.27 | convolution fusion | flops 2961178624 | bytes 9973760 | tf_op jit(solution)/shard_map/dot_general | solution.py:102
  277.8 12.4 %convolution_convert_fusion = bf16[1024,2048]{1,0:T(8,128)(2,1)} fusion(bf16[704,2048]{1,0:T(8,128)(2,1)} %param.25, f32[1024,704]{0,1:T(8,128)} %fusion.15, bf16[2048,704]{0,1:T(8,128)(2,1)} %param.24, bf16[1024,2048]{1,0:T(8,128)(2,1)} %all-gather.2.cloned.1.call-done, f32[2048]{0:T(1024)S(1)} %copy-done.12, f32[1024]{0:T(1024)S(1)} %add_rsqrt_fusion), kind=kOutput, calls=%fused_computation.20 | convolution fusion | flops 5920391168 | bytes 17051648 | tf_op jit(solution)/shard_map/dot_general | solution.py:106
  290.2 37.9 %reduce-scatter.2.cloned.1.call-done = bf16[128,2048]{1,0:T(8,128)(2,1)} async-done(((bf16[1024,2048]{1,0:T(8,128)(2,1)}), bf16[128,2048]{1,0:T(8,128)(2,1)}) %reduce-scatter.2.cloned.1.call-update) | async-done | bytes 524304 | tf_op jit(solution)/shard_map/reduce_scatter | solution.py:105
  331.1 52.8 %all_to_all.29 = bf16[8,128,2048]{2,1,0:T(8,128)(2,1)S(1)} all-to-all(bf16[8,128,2048]{2,1,0:T(8,128)(2,1)S(1)} %stack.2), channel_id=1, replica_groups=mesh['req'=8,'tok'=16] {'req'}, dimensions={0} | all-to-all | bytes 8388608 | tf_op jit(solution)/shard_map/all_to_all | solution.py:115
  383.9 4.5 convolution_convert_fusion.1
  388.5 4.3 all-to-all-start.1
  396.1 18.2 %all-to-all-done.1 = bf16[8,128,768]{2,1,0:T(8,128)(2,1)} async-done(((bf16[8,128,768]{2,1,0:T(8,128)(2,1)}), bf16[8,128,768]{2,1,0:T(8,128)(2,1)}, u32[]{:S(2)}, u32[]{:S(2)}) %all-to-all-start.1) | async-done | bytes 1572896 | tf_op jit(solution)/shard_map/all_to_all | solution.py:120
  418.1 2.8 gather_fusion.1
  420.9 7.0 %all-to-all-start.2 = ((bf16[16,1,8,4096]{3,2,1,0:T(8,128)(2,1)}), bf16[16,1,8,4096]{3,2,1,0:T(8,128)(2,1)}, u32[]{:S(2)}, u32[]{:S(2)}) async-start(bf16[16,1,8,4096]{3,2,1,0:T(8,128)(2,1)} %bitcast.68), calls=%async_computation.3 | async-start | bytes 2097152 | tf_op jit(solution)/shard_map/all_to_all | solution.py:131
  431.3 14.1 %all-to-all-done.2 = bf16[16,1,8,4096]{3,2,1,0:T(8,128)(2,1)} async-done(((bf16[16,1,8,4096]{3,2,1,0:T(8,128)(2,1)}), bf16[16,1,8,4096]{3,2,1,0:T(8,128)(2,1)}, u32[]{:S(2)}, u32[]{:S(2)}) %all-to-all-start.2) | async-done | bytes 1048608 | tf_op jit(solution)/shard_map/all_to_all | solution.py:131
  446.5 3.4 scatter_fusion
  (89 shorter events, 43.6 us)
Async XLA Ops:
  7.2 376.8 %copy-start = (bf16[2048,768]{1,0:T(8,128)(2,1)S(1)}, bf16[2048,768]{1,0:T(8,128)(2,1)}, u32[]{:S(2)}) copy-start(bf16[2048,768]{1,0:T(8,128)(2,1)} %param.27) | copy-start | bytes 9437188
  7.2 26.4 %copy-start.1 = (s32[1,2048]{1,0:T(1,128)S(1)}, s32[1,2048]{1,0:T(1,128)}, u32[]{:S(2)}) copy-start(s32[1,2048]{1,0:T(1,128)} %param.19) | copy-start | bytes 24580
  7.2 259.5 %all-gather.2.cloned.1.call-start = ((), (), s32[]{:S(2)}) async-start(), calls=%async_computation.4 | async-start | bytes 4718592 | tf_op jit(solution)/shard_map/all_gather | solution.py:100
  13.7 31.7 %collective-permute-start = (bf16[128,4096]{0,1:T(8,128)(2,1)}, bf16[128,4096]{0,1:T(8,128)(2,1)}, u32[]{:S(2)}, u32[]{:S(2)}) collective-permute-start(bf16[128,4096]{0,1:T(8,128)(2,1)} %pad_maximum_fusion), channel_id=1, source_target_pairs={{0,8},{1,9},{2,10},{3,11},{4,12},{5,13},{6,14},{7,15},{16,24},{17,... | collective-permute-start | bytes 3145736 | tf_op jit(solution)/shard_map/ppermute | solution.py:60
  19.7 45.4 %collective-permute-start.1 = (bf16[128,4096]{0,1:T(8,128)(2,1)}, bf16[128,4096]{0,1:T(8,128)(2,1)}, u32[]{:S(2)}, u32[]{:S(2)}) collective-permute-start(bf16[128,4096]{0,1:T(8,128)(2,1)} %pad_maximum_fusion), channel_id=1, source_target_pairs={{0,7},{1,8},{2,9},{3,10},{4,11},{5,12},{6,13},{7,14},{8,15},{16,23... | collective-permute-start | bytes 3145736 | tf_op jit(solution)/shard_map/ppermute | solution.py:60
  26.7 60.9 %collective-permute-start.2 = (bf16[128,4096]{0,1:T(8,128)(2,1)}, bf16[128,4096]{0,1:T(8,128)(2,1)}, u32[]{:S(2)}, u32[]{:S(2)}) collective-permute-start(bf16[128,4096]{0,1:T(8,128)(2,1)} %pad_maximum_fusion), channel_id=1, source_target_pairs={{0,6},{1,7},{2,8},{3,9},{4,10},{5,11},{6,12},{7,13},{8,14},{9,15},... | collective-permute-start | bytes 3145736 | tf_op jit(solution)/shard_map/ppermute | solution.py:60
  29.0 81.2 %collective-permute-start.3 = (bf16[128,4096]{0,1:T(8,128)(2,1)}, bf16[128,4096]{0,1:T(8,128)(2,1)}, u32[]{:S(2)}, u32[]{:S(2)}) collective-permute-start(bf16[128,4096]{0,1:T(8,128)(2,1)} %pad_maximum_fusion), channel_id=1, source_target_pairs={{0,5},{1,6},{2,7},{3,8},{4,9},{5,10},{6,11},{7,12},{8,13},{9,14},{... | collective-permute-start | bytes 3145736 | tf_op jit(solution)/shard_map/ppermute | solution.py:60
  31.2 100.2 %collective-permute-start.4 = (bf16[128,4096]{0,1:T(8,128)(2,1)}, bf16[128,4096]{0,1:T(8,128)(2,1)}, u32[]{:S(2)}, u32[]{:S(2)}) collective-permute-start(bf16[128,4096]{0,1:T(8,128)(2,1)} %pad_maximum_fusion), channel_id=1, source_target_pairs={{0,4},{1,5},{2,6},{3,7},{4,8},{5,9},{6,10},{7,11},{8,12},{9,13},{1... | collective-permute-start | bytes 3145736 | tf_op jit(solution)/shard_map/ppermute | solution.py:60
  33.6 9.8 %copy-start.9 = (f32[4,128]{1,0:T(4,128)S(1)}, f32[4,128]{1,0:T(4,128)}, u32[]{:S(2)}) copy-start(f32[4,128]{1,0:T(4,128)} %param.20) | copy-start | bytes 6148
  45.4 88.4 %collective-permute-start.5 = (bf16[128,4096]{0,1:T(8,128)(2,1)}, bf16[128,4096]{0,1:T(8,128)(2,1)S(1)}, u32[]{:S(2)}, u32[]{:S(2)}) collective-permute-start(bf16[128,4096]{0,1:T(8,128)(2,1)} %pad_maximum_fusion), channel_id=1, source_target_pairs={{0,3},{1,4},{2,5},{3,6},{4,7},{5,8},{6,9},{7,10},{8,11},{9,12},{10... | collective-permute-start | bytes 3145736 | tf_op jit(solution)/shard_map/ppermute | solution.py:60
  65.1 69.8 %collective-permute-start.6 = (bf16[128,4096]{0,1:T(8,128)(2,1)}, bf16[128,4096]{0,1:T(8,128)(2,1)S(1)}, u32[]{:S(2)}, u32[]{:S(2)}) collective-permute-start(bf16[128,4096]{0,1:T(8,128)(2,1)} %pad_maximum_fusion), channel_id=1, source_target_pairs={{0,2},{1,3},{2,4},{3,5},{4,6},{5,7},{6,8},{7,9},{8,10},{9,11},{10,... | collective-permute-start | bytes 3145736 | tf_op jit(solution)/shard_map/ppermute | solution.py:60
  87.6 48.4 %collective-permute-start.7 = (bf16[128,4096]{0,1:T(8,128)(2,1)}, bf16[128,4096]{0,1:T(8,128)(2,1)S(1)}, u32[]{:S(2)}, u32[]{:S(2)}) collective-permute-start(bf16[128,4096]{0,1:T(8,128)(2,1)} %pad_maximum_fusion), channel_id=1, source_target_pairs={{0,1},{1,2},{2,3},{3,4},{4,5},{5,6},{6,7},{7,8},{8,9},{9,10},{10,1... | collective-permute-start | bytes 3145736 | tf_op jit(solution)/shard_map/ppermute | solution.py:60
  112.5 24.7 %copy-start.4 = (bf16[128,2048]{0,1:T(8,128)(2,1)S(1)}, bf16[128,2048]{0,1:T(8,128)(2,1)}, u32[]{:S(2)}) copy-start(bf16[128,2048]{0,1:T(8,128)(2,1)} %copy.38) | copy-start | bytes 1572868
  112.5 24.7 %copy-start.5 = (bf16[128,2048]{0,1:T(8,128)(2,1)S(1)}, bf16[128,2048]{0,1:T(8,128)(2,1)}, u32[]{:S(2)}) copy-start(bf16[128,2048]{0,1:T(8,128)(2,1)} %copy.39) | copy-start | bytes 1572868
  138.3 6.8 %copy-start.6 = (bf16[128,8,2,128]{3,2,1,0:T(2,128)(2,1)S(1)}, bf16[128,8,2,128]{3,2,1,0:T(2,128)(2,1)}, u32[]{:S(2)}) copy-start(bf16[128,8,2,128]{3,2,1,0:T(2,128)(2,1)} %reshape.146) | copy-start | bytes 1572868
  147.6 3.6 copy-start.2
  168.5 101.3 %copy-start.12 = (f32[2048]{0:T(1024)S(1)}, f32[2048]{0:T(1024)}, u32[]{:S(2)}) copy-start(f32[2048]{0:T(1024)} %param.22) | copy-start | bytes 24580
  168.5 159.6 %reduce-scatter.2.cloned.1.call-start = ((), (), s32[]{:S(2)}) async-start(), calls=%async_computation.5 | async-start | bytes 4718592 | tf_op jit(solution)/shard_map/reduce_scatter | solution.py:105
  290.2 40.2 %copy-start.8 = (f32[2048]{0:T(1024)S(1)}, f32[2048]{0:T(1024)}, u32[]{:S(2)}) copy-start(f32[2048]{0:T(1024)} %param.26) | copy-start | bytes 24580
  329.6 0.8 copy-start.7
  383.9 9.3 %copy-start.10 = (s32[1,256]{1,0:T(1,128)S(1)}, s32[1,256]{1,0:T(1,128)}, u32[]{:S(2)}) copy-start(s32[1,256]{1,0:T(1,128)} %param.28) | copy-start | bytes 3076
  383.9 10.2 %copy-start.11 = (s32[1,256]{1,0:T(1,128)S(1)}, s32[1,256]{1,0:T(1,128)}, u32[]{:S(2)}) copy-start(s32[1,256]{1,0:T(1,128)} %param.29) | copy-start | bytes 3076
  388.5 25.9 %all-to-all-start.1 = ((bf16[8,128,768]{2,1,0:T(8,128)(2,1)}), bf16[8,128,768]{2,1,0:T(8,128)(2,1)}, u32[]{:S(2)}, u32[]{:S(2)}) async-start(bf16[8,128,768]{2,1,0:T(8,128)(2,1)} %bitcast.71), calls=%async_computation.2 | async-start | bytes 3145728 | tf_op jit(solution)/shard_map/all_to_all | solution.py:120
  415.9 1.2 copy-start.3
  420.9 24.5 %all-to-all-start.2 = ((bf16[16,1,8,4096]{3,2,1,0:T(8,128)(2,1)}), bf16[16,1,8,4096]{3,2,1,0:T(8,128)(2,1)}, u32[]{:S(2)}, u32[]{:S(2)}) async-start(bf16[16,1,8,4096]{3,2,1,0:T(8,128)(2,1)} %bitcast.68), calls=%async_computation.3 | async-start | bytes 2097152 | tf_op jit(solution)/shard_map/all_to_all | solution.py:131
Sparse Core Ops, SparseCore 0:
  168.7 98.0 all-gather.1
  290.4 37.7 reduce-scatter.1
